TPU v7x, 32 devices: a whole 2x2x4 slice. The times are simulated.
32 devices in a mesh: dp: 8 (over z, x), head: 4 (over y, core).
Axes of the slice: x: 2, y: 2, z: 4, core: 2. Of those that a mesh axis runs over, the one named last changes fastest.
Arguments:
- layer_input: bfloat16 [64, 197, 768], P(('dp', 'head')), may hold values from -6 to 6
- prompts: bfloat16 [100, 768], replicated, may hold values from -6 to 6
- lengths: int32 [64], P('dp'), may hold values from 1 to 100, as said below
- key_mask: int32 [64, 297], P('dp'), may hold values 0 or 1
- ln1_gain: float32 [768], replicated, may hold values from 0.1 to 1.9
- ln1_shift: float32 [768], replicated, may hold values from -1.5 to 1.5
- w_qkv: bfloat16 [3, 768, 768], P(None, 'dp', 'head'), may hold values from -0.3125 to 0.3125
- w_out: bfloat16 [768, 768], P('head', 'dp'), may hold values from -0.875 to 0.875
- b_out: float32 [768], replicated, may hold values from -1.5 to 1.5
- ln2_gain: float32 [768], replicated, may hold values from 0.1 to 1.9
- ln2_shift: float32 [768], replicated, may hold values from -1.5 to 1.5
- w_fc1: bfloat16 [768, 3072], P('dp', 'head'), may hold values from -0.21875 to 0.21875
- b_fc1: float32 [3072], P('head'), may hold values from -2.5 to 2.5
- w_fc2: bfloat16 [3072, 768], P('head', 'dp'), may hold values from -0.15625 to 0.15625
- b_fc2: float32 [768], replicated, may hold values from -1.5 to 1.5
- grad_output: bfloat16 [64, 297, 768], P(('dp', 'head')), may hold values from -6 to 6
Outputs:
- layer_output: bfloat16 [64, 297, 768], P(('dp', 'head'))
- grad_input: bfloat16 [64, 197, 768], P(('dp', 'head'))
- grad_prompts: float32 [100, 768], replicated
Inputs may be any that keep to these rules, and one draw needn't show every extreme that they name: `lengths`: each length is one of 1, 10, 50 and 100; both 1 and 100 occur.
All inputs are finite; a program needn't handle non-finite values. No bound on the sum of `key_mask` on one device may be relied on, other than what follows from the above.
Results may differ from a plain program's by a relative error of at most 0.019.
Values may be sent and summed in bfloat16 or wider, within the bound.
No kernel may reach another device: no remote copies, remote signals or barrier semaphores. Data moves between devices by JAX's collectives and lax.ppermute only.
A program may use at most 128 MiB of HBM per device.

v0:
```python
import jax
import jax.numpy as jnp
from jax import lax
from jax.sharding import PartitionSpec as P

HEAD_DIM = 64
IMG_TOK = 197
PROMPTS = 100
EPSILON = 1e-06


def layer_norm(rows, gain, shift):
    center = rows - jnp.mean(rows, axis=-1, keepdims=True)
    return (
        center * lax.rsqrt(jnp.mean(center * center, axis=-1, keepdims=True) + EPSILON) * gain
        + shift
    )


def token_masks(lengths, key_mask):
    position = lax.broadcasted_iota(jnp.int32, key_mask.shape, 1)
    used = (position < IMG_TOK) | (position - IMG_TOK < lengths[:, None])
    seen = (key_mask == 1) | (position == 0)
    return (used, used & seen)


def project(rows_b, weight):
    return jnp.einsum("isd,dc->isc", rows_b, weight, preferred_element_type=jnp.float32)


def attend(rows_b, full_qkv, visible):
    img_count, seq_len = (rows_b.shape[0], rows_b.shape[1])
    head_count = full_qkv.shape[2] // HEAD_DIM
    projected = jnp.einsum(
        "isd,tdc->tisc", rows_b, full_qkv, preferred_element_type=jnp.float32
    ).astype(jnp.bfloat16)
    projected = projected.reshape(3, img_count, seq_len, head_count, HEAD_DIM)
    query_rows, key_rows, value_rows = (projected[0], projected[1], projected[2])
    scores = jnp.einsum(
        "ishc,ithc->ihst", query_rows, key_rows, preferred_element_type=jnp.float32
    ) * HEAD_DIM ** (-0.5)
    scores = jnp.where(visible[:, None, None, :], scores, -1000000000.0)
    attn_probs = jax.nn.softmax(scores, axis=-1)
    return (query_rows, key_rows, value_rows, attn_probs)


def mix_values(probs_b, value_rows):
    img_count, seq_len = (value_rows.shape[0], value_rows.shape[1])
    context = jnp.einsum("ihst,ithc->ishc", probs_b, value_rows, preferred_element_type=jnp.float32)
    return context.astype(jnp.bfloat16).reshape(img_count, seq_len, value_rows.shape[2] * HEAD_DIM)


def mlp_back(grad_all, pre_act, fc1_rows, fc2_rows):
    grad_active_b = jnp.einsum(
        "isd,fd->isf", grad_all, fc2_rows, preferred_element_type=jnp.float32
    ).astype(jnp.bfloat16)
    _, gelu_back = jax.vjp(lambda values_in: jax.nn.gelu(values_in, approximate=False), pre_act)
    grad_pre_b = gelu_back(grad_active_b.astype(jnp.float32))[0].astype(jnp.bfloat16)
    return jnp.einsum("isf,df->isd", grad_pre_b, fc1_rows, preferred_element_type=jnp.float32)


def attn_back(grad_all, out_rows, qkv_rows, query_rows, key_rows, value_rows, attn_probs, probs_b):
    img_count, seq_len, head_count = (value_rows.shape[0], value_rows.shape[1], value_rows.shape[2])
    local_width = head_count * HEAD_DIM
    grad_context = jnp.einsum(
        "isd,cd->isc", grad_all, out_rows, preferred_element_type=jnp.float32
    ).astype(jnp.bfloat16)
    grad_context = grad_context.reshape(img_count, seq_len, head_count, HEAD_DIM)
    grad_value = jnp.einsum(
        "ihst,ishc->ithc", probs_b, grad_context, preferred_element_type=jnp.float32
    ).astype(jnp.bfloat16)
    grad_probs = jnp.einsum(
        "ishc,ithc->ihst", grad_context, value_rows, preferred_element_type=jnp.float32
    )
    grad_scores = (
        attn_probs * (grad_probs - jnp.sum(attn_probs * grad_probs, axis=-1, keepdims=True))
    ).astype(jnp.bfloat16)
    grad_query = (
        jnp.einsum("ihst,ithc->ishc", grad_scores, key_rows, preferred_element_type=jnp.float32)
        * HEAD_DIM ** (-0.5)
    ).astype(jnp.bfloat16)
    grad_key = (
        jnp.einsum("ihst,ishc->ithc", grad_scores, query_rows, preferred_element_type=jnp.float32)
        * HEAD_DIM ** (-0.5)
    ).astype(jnp.bfloat16)
    stacked = jnp.stack([grad_query, grad_key, grad_value]).reshape(
        3, img_count, seq_len, local_width
    )
    return jnp.einsum("tisc,tdc->isd", stacked, qkv_rows, preferred_element_type=jnp.float32)


def per_device(
    layer_input,
    prompts,
    lengths,
    key_mask,
    ln1_gain,
    ln1_shift,
    w_qkv,
    w_out,
    b_out,
    ln2_gain,
    ln2_shift,
    w_fc1,
    b_fc1,
    w_fc2,
    b_fc2,
    grad_output,
):
    own_count = layer_input.shape[0]
    model_width = layer_input.shape[2]
    offset = lax.axis_index("head") * own_count
    used_all, visible = token_masks(lengths, key_mask)
    used_own = lax.dynamic_slice_in_dim(used_all, offset, own_count, 0).astype(jnp.float32)[
        ..., None
    ]
    gain_one, shift_one = (ln1_gain, ln1_shift)
    gain_two, shift_two = (ln2_gain, ln2_shift)
    full_qkv, full_out, full_fc1, full_fc2 = (
        lax.all_gather(w_qkv, "dp", axis=1, tiled=True),
        lax.all_gather(w_out, "dp", axis=1, tiled=True),
        lax.all_gather(w_fc1, "dp", axis=0, tiled=True),
        lax.all_gather(w_fc2, "dp", axis=1, tiled=True),
    )
    prompt_rows = jnp.broadcast_to(
        prompts.astype(jnp.float32)[None], (own_count, PROMPTS, model_width)
    )
    stream = jnp.concatenate([layer_input.astype(jnp.float32), prompt_rows], axis=1)
    normed_attn, back_attn_norm = jax.vjp(
        lambda rows: layer_norm(rows, gain_one, shift_one), stream
    )
    normed_attn_b = normed_attn.astype(jnp.bfloat16)
    grad_rows = grad_output.astype(jnp.float32) * used_own
    gathered_attn = lax.all_gather(normed_attn_b, "head", axis=0, tiled=True)
    query_rows, key_rows, value_rows, attn_probs = attend(gathered_attn, full_qkv, visible)
    probs_b = attn_probs.astype(jnp.bfloat16)
    context = mix_values(probs_b, value_rows)
    attn_sum = lax.psum_scatter(
        project(context, full_out).astype(jnp.bfloat16), "head", scatter_dimension=0, tiled=True
    ).astype(jnp.float32)
    hidden_mid = stream + attn_sum + b_out
    normed_mlp, back_mlp_norm = jax.vjp(
        lambda rows: layer_norm(rows, gain_two, shift_two), hidden_mid
    )
    normed_mlp_b = normed_mlp.astype(jnp.bfloat16)
    gathered_mlp = lax.all_gather(normed_mlp_b, "head", axis=0, tiled=True)
    pre_act = project(gathered_mlp, full_fc1) + b_fc1
    active_b = jax.nn.gelu(pre_act, approximate=False).astype(jnp.bfloat16)
    mlp_sum = lax.psum_scatter(
        project(active_b, full_fc2).astype(jnp.bfloat16), "head", scatter_dimension=0, tiled=True
    ).astype(jnp.float32)
    result = ((hidden_mid + mlp_sum + b_fc2) * used_own).astype(jnp.bfloat16)
    held_inputs = lax.optimization_barrier((w_qkv, w_out, w_fc1, w_fc2, grad_rows))
    grad_rows = held_inputs[4]
    back_qkv, back_out, back_fc1, back_fc2 = (
        lax.all_gather(held_inputs[0], "dp", axis=1, tiled=True),
        lax.all_gather(held_inputs[1], "dp", axis=1, tiled=True),
        lax.all_gather(held_inputs[2], "dp", axis=0, tiled=True),
        lax.all_gather(held_inputs[3], "dp", axis=1, tiled=True),
    )
    grad_mlp_b = grad_rows.astype(jnp.bfloat16)
    grad_mlp_all, gathered_again = (
        lax.all_gather(grad_mlp_b, "head", axis=0, tiled=True),
        lax.all_gather(normed_mlp_b, "head", axis=0, tiled=True),
    )
    pre_act = project(gathered_again, back_fc1) + b_fc1
    grad_normed_mlp = lax.psum_scatter(
        mlp_back(grad_mlp_all, pre_act, back_fc1, back_fc2).astype(jnp.bfloat16),
        "head",
        scatter_dimension=0,
        tiled=True,
    ).astype(jnp.float32)
    grad_mid = grad_rows + back_mlp_norm(grad_normed_mlp)[0]
    grad_attn_b = grad_mid.astype(jnp.bfloat16)
    grad_attn_all, gathered_again = (
        lax.all_gather(grad_attn_b, "head", axis=0, tiled=True),
        lax.all_gather(normed_attn_b, "head", axis=0, tiled=True),
    )
    query_rows, key_rows, value_rows, attn_probs = attend(gathered_again, back_qkv, visible)
    probs_b = attn_probs.astype(jnp.bfloat16)
    grad_partial = attn_back(
        grad_attn_all, back_out, back_qkv, query_rows, key_rows, value_rows, attn_probs, probs_b
    )
    grad_normed_attn = lax.psum_scatter(
        grad_partial.astype(jnp.bfloat16), "head", scatter_dimension=0, tiled=True
    ).astype(jnp.float32)
    grad_stream = grad_mid + back_attn_norm(grad_normed_attn)[0]
    grad_input = grad_stream[:, :IMG_TOK].astype(jnp.bfloat16)
    grad_prompts = lax.psum(jnp.sum(grad_stream[:, IMG_TOK:], axis=0), ("dp", "head"))
    return (result, grad_input, grad_prompts)


def solution(mesh):
    placed = (
        P(("dp", "head"), None, None),
        P(),
        P("dp"),
        P("dp", None),
        P(),
        P(),
        P(None, "dp", "head"),
        P("head", "dp"),
        P(),
        P(),
        P(),
        P("dp", "head"),
        P("head"),
        P("head", "dp"),
        P(),
        P(("dp", "head"), None, None),
    )
    return jax.shard_map(
        per_device,
        mesh=mesh,
        in_specs=placed,
        out_specs=(P(("dp", "head"), None, None), P(("dp", "head"), None, None), P()),
        check_vma=False,
    )
```

profile of v0, /device:TPU:8, one launch (start us, length us, event | category | flops | bytes accessed | tf_op | source)
XLA Modules:
  0.0 717.3 jit_solution(3644398181313778874)
XLA Ops:
  12.6 36.7 %all_gather.39 = bf16[3,768,192]{2,0,1:T(4,128)(2,1)} all-gather(bf16[3,96,192]{2,0,1:T(4,128)(2,1)S(1)} %copy.34), channel_id=1, replica_groups=mesh['dp'=8,'head'=4] {'dp'}, dimensions={1}, use_global_device_ids=true | all-gather | bytes 995328 | tf_op jit(solution)/shard_map/all_gather | solution.py:120
  52.7 30.5 %all_gather.40 = bf16[192,768]{0,1:T(8,128)(2,1)S(1)} all-gather(bf16[192,96]{0,1:T(8,128)(2,1)S(1)} %copy.37), channel_id=1, replica_groups=mesh['dp'=8,'head'=4] {'dp'}, dimensions={1}, use_global_device_ids=true | all-gather | bytes 331776 | tf_op jit(solution)/shard_map/all_gather | solution.py:121
  90.5 8.2 %fusion.168 = (f32[8,3,297]{2,1,0:T(4,128)S(1)}, f32[8,3,297,297]{2,3,1,0:T(8,128)}) fusion(pred[8,297]{1,0:T(8,128)(4,1)S(1)} %get-tuple-element.30, bf16[8,297,3,64]{1,3,2,0:T(8,128)(2,1)} %bitcast.105, bf16[8,297,3,64]{1,3,2,0:T(8,128)(2,1)} %bitcast.104), kind=kOutput, calls=%fused_computation.222 | convolution fusion | flops 279446432 | bytes 10323720 | tf_op jit(solution)/shard_map/sub | solution.py:43
  98.7 5.8 fusion.73
  110.4 41.4 %reduce-scatter.5.cloned.1.call-done = bf16[2,297,768]{2,1,0:T(8,128)(2,1)} async-done(((bf16[8,297,768]{2,1,0:T(8,128)(2,1)}), bf16[2,297,768]{2,1,0:T(8,128)(2,1)}) %reduce-scatter.5.cloned.1.call-update) | async-done | bytes 912400 | tf_op jit(solution)/shard_map/reduce_scatter | solution.py:138
  161.7 26.8 %all-gather.11.cloned.1.call-done = bf16[8,297,768]{2,1,0:T(8,128)(2,1)} async-done(((bf16[2,297,768]{2,1,0:T(8,128)(2,1)}), bf16[8,297,768]{2,1,0:T(8,128)(2,1)}) %all-gather.11.cloned.1.call-update) | async-done | bytes 3649552 | tf_op jit(solution)/shard_map/all_gather | solution.py:146
  188.5 8.4 %fusion.82 = f32[8,297,768]{2,1,0:T(8,128)} fusion(bf16[8,297,768]{2,1,0:T(8,128)(2,1)} %all-gather.11.cloned.1.call-done, bf16[768,768]{1,0:T(8,128)(2,1)} %all-gather.17.cloned.1.call-done), kind=kOutput, calls=%fused_computation.120 | convolution fusion | flops 2802843648 | bytes 12128256 | tf_op jit(solution)/shard_map/isd,dc->isc/dot_general | solution.py:28
  196.9 34.4 %all-gather.21.cloned.1.call-done = bf16[768,768]{0,1:T(8,128)(2,1)} async-done(((bf16[768,96]{0,1:T(8,128)(2,1)}), bf16[768,768]{0,1:T(8,128)(2,1)}) %all-gather.21.cloned.1.call-update) | async-done | bytes 1179664 | tf_op jit(solution)/shard_map/all_gather | solution.py:159
  231.3 32.9 %all-gather.19.cloned.1.call-done = bf16[8,297,768]{2,1,0:T(8,128)(2,1)} async-done(((bf16[2,297,768]{2,1,0:T(8,128)(2,1)}), bf16[8,297,768]{2,1,0:T(8,128)(2,1)}) %all-gather.19.cloned.1.call-update) | async-done | bytes 3649552 | tf_op jit(solution)/shard_map/all_gather | solution.py:163
  264.2 27.0 %fusion.57 = bf16[8,297,768]{2,1,0:T(8,128)(2,1)} fusion(f32[8,297,768]{2,1,0:T(8,128)} %fusion.82, f32[768]{0:T(1024)S(1)} %copy-done.35, bf16[8,297,768]{2,1,0:T(8,128)(2,1)} %all-gather.19.cloned.1.call-done, bf16[768,768]{0,1:T(8,128)(2,1)} %all-gather.21.cloned.1.call-done, bf16[768,768]{1,0:T(8,128)(2,1)} %all-gather.17.cloned.1.call-done), kind=kOutput, calls=%fused_computation.89 | convolution fusion | flops 5744369664 | bytes 16960512 | tf_op jit(solution)/shard_map/isf,df->isd/dot_general | solution.py:59
  291.2 9.2 %reduce-scatter.7.cloned.1.call-start = ((), (), s32[]{:S(2)}) async-start(), calls=%async_computation.9 | async-start | bytes 4669440 | tf_op jit(solution)/shard_map/reduce_scatter | solution.py:149
  300.4 6.6 all-gather.13.cloned.1.call-done
  307.0 10.3 %fusion.70 = (u8[297,768]{1,0:T(8,128)(4,1)S(1)}, u8[297,768]{1,0:T(8,128)(4,1)S(1)}, f32[8,297,768]{2,1,0:T(8,128)}) fusion(f32[768]{0:T(1024)S(1)} %copy-done.35, bf16[8,297,768]{2,1,0:T(8,128)(2,1)} %all-gather.11.cloned.1.call-done, bf16[768,768]{1,0:T(8,128)(2,1)} %all-gather.13.cloned.1.call-done), kind=kOutput, calls=%fused_computation.109 | convolution fusion | flops 2827934208 | bytes 12587520 | tf_op jit(solution)/shard_map/isd,dc->isc/dot_general | solution.py:28
  317.2 32.0 %all-gather.15.cloned.1.call-done = bf16[768,768]{0,1:T(8,128)(2,1)} async-done(((bf16[768,96]{0,1:T(8,128)(2,1)}), bf16[768,768]{0,1:T(8,128)(2,1)}) %all-gather.15.cloned.1.call-update) | async-done | bytes 1179664 | tf_op jit(solution)/shard_map/all_gather | solution.py:123
  349.3 23.0 %fusion.60 = bf16[8,297,768]{2,1,0:T(8,128)(2,1)} fusion(f32[8,297,768]{2,1,0:T(8,128)} %get-tuple-element.33, f32[768]{0:T(1024)S(1)} %copy-done.35, bf16[768,768]{0,1:T(8,128)(2,1)} %all-gather.15.cloned.1.call-done, u8[297,768]{1,0:T(8,128)(4,1)S(1)} %get-tuple-element.20, u8[297,768]{1,0:T(8,128)(4,1)S(1)} %get-tuple-element.19), kind=kOutput, calls=%fused_computation.90 | convolution fusion | flops 2934226944 | bytes 12587520 | tf_op jit(solution)/shard_map/isd,dc->isc/dot_general | solution.py:28
  375.4 38.2 %reduce-scatter.7.cloned.1.call-done = bf16[2,297,768]{2,1,0:T(8,128)(2,1)} async-done(((bf16[8,297,768]{2,1,0:T(8,128)(2,1)}), bf16[2,297,768]{2,1,0:T(8,128)(2,1)}) %reduce-scatter.7.cloned.1.call-update) | async-done | bytes 912400 | tf_op jit(solution)/shard_map/reduce_scatter | solution.py:149
  417.5 28.5 %all_gather.49 = bf16[192,768]{0,1:T(8,128)(2,1)S(1)} all-gather(bf16[192,96]{0,1:T(8,128)(2,1)S(1)} %copy.42), channel_id=1, replica_groups=mesh['dp'=8,'head'=4] {'dp'}, dimensions={1}, use_global_device_ids=true | all-gather | bytes 331776 | tf_op jit(solution)/shard_map/all_gather | solution.py:157
  446.1 39.4 %all_gather.47 = bf16[3,768,192]{2,0,1:T(4,128)(2,1)S(1)} all-gather(bf16[3,96,192]{2,0,1:T(4,128)(2,1)S(1)} %copy.40), channel_id=1, replica_groups=mesh['dp'=8,'head'=4] {'dp'}, dimensions={1}, use_global_device_ids=true | all-gather | bytes 995328 | tf_op jit(solution)/shard_map/all_gather | solution.py:156
  485.5 7.7 %convert_bitcast_fusion = bf16[3,8,297,192]{2,3,1,0:T(8,128)(2,1)S(1)} fusion(bf16[8,297,768]{2,1,0:T(8,128)(2,1)} %all-gather.9.cloned.1.call-done, bf16[3,768,192,1]{2,0,1,3:T(4,128)(2,1)S(1)} %bitcast.101), kind=kOutput, calls=%fused_computation.84 | convolution fusion | flops 2103501312 | bytes 7271424 | tf_op jit(solution)/shard_map/isd,tdc->tisc/dot_general | solution.py:34
  495.2 8.2 %fusion.169 = (f32[8,3,297]{2,1,0:T(4,128)S(1)}, f32[8,3,297,297]{2,3,1,0:T(8,128)}) fusion(pred[8,297]{1,0:T(8,128)(4,1)S(1)} %copy-done.33, bf16[8,297,3,64]{1,3,2,0:T(8,128)(2,1)} %bitcast.98, bf16[8,297,3,64]{1,3,2,0:T(8,128)(2,1)} %bitcast.96), kind=kOutput, calls=%fused_computation.223 | convolution fusion | flops 279446432 | bytes 10323720 | tf_op jit(solution)/shard_map/sub | solution.py:43
  507.1 7.6 %fusion.74 = bf16[8,3,64,297]{3,2,1,0:T(8,128)(2,1)} fusion(bf16[8,297,3,64]{1,3,2,0:T(8,128)(2,1)S(1)} %bitcast.109, f32[8,3,297,297]{2,3,1,0:T(8,128)} %get-tuple-element.35, f32[8,3,297]{2,1,0:T(4,128)S(1)} %get-tuple-element.34), kind=kOutput, calls=%fused_computation.113 | convolution fusion | flops 275668288 | bytes 10321344 | tf_op jit(solution)/shard_map/ihst,ishc->ithc/dot_general | solution.py:69
  525.0 5.4 bitcast_convert_fusion
  530.5 42.3 %reduce-scatter.11.cloned.1.call-done = bf16[2,297,768]{2,1,0:T(8,128)(2,1)} async-done(((bf16[8,297,768]{2,1,0:T(8,128)(2,1)}), bf16[2,297,768]{2,1,0:T(8,128)(2,1)}) %reduce-scatter.11.cloned.1.call-update) | async-done | bytes 912400 | tf_op jit(solution)/shard_map/reduce_scatter | solution.py:184
  585.8 122.2 %all-reduce.2.cloned.1.call-done = f32[100,768]{1,0:T(8,128)} async-done(((f32[100,768]{1,0:T(8,128)}), f32[100,768]{1,0:T(8,128)}) %all-reduce.2.cloned.1.call-update) | async-done | bytes 307216 | tf_op jit(solution)/shard_map/psum | solution.py:189
  (159 shorter events, 68.2 us)
Async XLA Ops:
  8.0 75.3 %all-gather.9.cloned.1.call-start = ((), (), s32[]{:S(2)}) async-start(), calls=%async_computation.4 | async-start | bytes 4669440 | tf_op jit(solution)/shard_map/all_gather | solution.py:134
  12.2 71.0 %copy-start.28 = (s32[8,297]{1,0:T(8,128)S(1)}, s32[8,297]{1,0:T(8,128)}, u32[]{:S(2)}) copy-start(s32[8,297]{1,0:T(8,128)} %param.19) | copy-start | bytes 28516
  12.2 71.0 %copy-start.34 = (s32[8]{0:T(128)S(1)}, s32[8]{0:T(128)}, u32[]{:S(2)}) copy-start(s32[8]{0:T(128)} %param.18) | copy-start | bytes 100
  12.2 139.5 %reduce-scatter.5.cloned.1.call-start = ((), (), s32[]{:S(2)}) async-start(), calls=%async_computation.5 | async-start | bytes 4669440 | tf_op jit(solution)/shard_map/reduce_scatter | solution.py:138
  107.7 44.1 %copy-start.12 = (f32[768]{0:T(1024)S(1)}, f32[768]{0:T(1024)}, u32[]{:S(2)}) copy-start(f32[768]{0:T(1024)} %param.24) | copy-start | bytes 9220
  107.7 54.0 %all-gather.17.cloned.1.call-start = ((), (), s32[]{:S(2)}) async-start(), calls=%async_computation.10 | async-start | bytes 1327104 | tf_op jit(solution)/shard_map/all_gather | solution.py:158
  110.3 44.8 %copy-start.17 = (f32[768]{0:T(1024)S(1)}, f32[768]{0:T(1024)}, u32[]{:S(2)}) copy-start(f32[768]{0:T(1024)} %param.25) | copy-start | bytes 9220
  110.3 44.8 %copy-start.30 = (f32[768]{0:T(1024)S(1)}, f32[768]{0:T(1024)}, u32[]{:S(2)}) copy-start(f32[768]{0:T(1024)} %param.26) | copy-start | bytes 9220
  110.3 78.1 %all-gather.11.cloned.1.call-start = ((), (), s32[]{:S(2)}) async-start(), calls=%async_computation.6 | async-start | bytes 4669440 | tf_op jit(solution)/shard_map/all_gather | solution.py:146
  156.6 74.7 %all-gather.21.cloned.1.call-start = ((), (), s32[]{:S(2)}) async-start(), calls=%async_computation.12 | async-start | bytes 1327104 | tf_op jit(solution)/shard_map/all_gather | solution.py:159
  157.2 107.0 %all-gather.19.cloned.1.call-start = ((), (), s32[]{:S(2)}) async-start(), calls=%async_computation.11 | async-start | bytes 4669440 | tf_op jit(solution)/shard_map/all_gather | solution.py:163
  159.9 147.1 %all-gather.13.cloned.1.call-start = ((), (), s32[]{:S(2)}) async-start(), calls=%async_computation.7 | async-start | bytes 1327104 | tf_op jit(solution)/shard_map/all_gather | solution.py:122
  160.6 188.6 %all-gather.15.cloned.1.call-start = ((), (), s32[]{:S(2)}) async-start(), calls=%async_computation.8 | async-start | bytes 1327104 | tf_op jit(solution)/shard_map/all_gather | solution.py:123
  161.4 102.9 %copy-start.35 = (f32[768]{0:T(1024)S(1)}, f32[768]{0:T(1024)}, u32[]{:S(2)}) copy-start(f32[768]{0:T(1024)} %param.28) | copy-start | bytes 9220
  161.4 211.0 %reduce-scatter.9.cloned.1.call-start = ((), (), s32[]{:S(2)}) async-start(), calls=%async_computation.13 | async-start | bytes 4669440 | tf_op jit(solution)/shard_map/reduce_scatter | solution.py:167
  291.2 122.4 %reduce-scatter.7.cloned.1.call-start = ((), (), s32[]{:S(2)}) async-start(), calls=%async_computation.9 | async-start | bytes 4669440 | tf_op jit(solution)/shard_map/reduce_scatter | solution.py:149
  372.3 131.1 %all-gather.23.cloned.1.call-start = ((), (), s32[]{:S(2)}) async-start(), calls=%async_computation.14 | async-start | bytes 4669440 | tf_op jit(solution)/shard_map/all_gather | solution.py:176
  375.4 42.0 %copy-start.11 = (bf16[3,96,192]{2,1,0:T(8,128)(2,1)S(1)}, bf16[3,96,192]{2,1,0:T(8,128)(2,1)}, u32[]{:S(2)}) copy-start(bf16[3,96,192]{2,1,0:T(8,128)(2,1)} %param.22) | copy-start | bytes 331780
  417.2 155.5 %reduce-scatter.11.cloned.1.call-start = ((), (), s32[]{:S(2)}) async-start(), calls=%async_computation.15 | async-start | bytes 4669440 | tf_op jit(solution)/shard_map/reduce_scatter | solution.py:184
  530.4 42.4 %copy-start.16 = (f32[2,297]{1,0:T(2,128)S(1)}, f32[2,297]{1,0:T(2,128)}, u32[]{:S(2)}) copy-start(f32[2,297]{1,0:T(2,128)} %copy-done.15) | copy-start | bytes 7132
  530.4 42.4 %copy-start.19 = (f32[768]{0:T(1024)S(1)}, f32[768]{0:T(1024)}, u32[]{:S(2)}) copy-start(f32[768]{0:T(1024)} %param.20) | copy-start | bytes 9220
  530.4 44.2 %copy-start.25 = (f32[2,297]{1,0:T(2,128)S(1)}, f32[2,297]{1,0:T(2,128)}, u32[]{:S(2)}) copy-start(f32[2,297]{1,0:T(2,128)} %copy-done.24) | copy-start | bytes 7132
  530.4 44.2 %copy-start.21 = (f32[2,297]{1,0:T(2,128)S(1)}, f32[2,297]{1,0:T(2,128)}, u32[]{:S(2)}) copy-start(f32[2,297]{1,0:T(2,128)} %copy-done.20) | copy-start | bytes 7132
  530.4 177.6 %all-reduce.2.cloned.1.call-start = ((), (), s32[]{:S(2)}) async-start(), calls=%async_computation.16 | async-start | bytes 638976 | tf_op jit(solution)/shard_map/psum | solution.py:189
  (30 other events, 224.9 us)
Sparse Core Ops, SparseCore 0:
  12.4 33.0 all-gather.8
  107.8 43.8 reduce-scatter.4
  291.3 41.6 reduce-scatter.8
  372.4 41.1 reduce-scatter.6
  580.5 127.5 all-reduce.1
Sparse Core Ops, SparseCore 1:
  110.6 42.7 all-gather.16
  156.7 31.7 all-gather.10
  190.8 40.5 all-gather.20
  233.0 31.2 all-gather.18
  266.4 40.5 all-gather.12
  309.2 40.0 all-gather.14
  417.3 31.7 all-gather.22
  530.5 42.2 reduce-scatter.10
where the time goes:
time: 726 us; the launch traced here: 717 us
  waiting for transfers between devices  379 us (52%)
  blocking collectives  135 us (19%)
  matrix products  132 us (18%)
  other arithmetic  26.4 us (4%)
  local copies, waits for them, and re-layouts  18.9 us (3%)
  between operations  16.4 us (2%)
  starting transfers between devices  9.95 us (1%)
    psum x1, waiting for transfers between devices, per_device(): lax.psum(jnp.sum(grad_stream[:, IMG_TOK:], axis=0), ('dp', 'head'))  122 us
    dot_general x4, matrix products, project(): jnp.einsum('isd,dc->isc', rows_b, weight, preferred_element_type=jnp.floa...  44.9 us
    reduce_scatter x1, waiting for transfers between devices, per_device(): lax.psum_scatter(grad_partial.astype(jnp.bfloat16), 'head', scatter_dimen...  42.3 us
    reduce_scatter x1, waiting for transfers between devices, per_device(): lax.psum_scatter(project(context, full_out).astype(jnp.bfloat16), 'head',...  41.4 us
    all_gather x1, blocking collectives, per_device(): lax.all_gather(held_inputs[0], 'dp', axis=1, tiled=True)  39.4 us
    reduce_scatter x1, waiting for transfers between devices, per_device(): lax.psum_scatter(project(active_b, full_fc2).astype(jnp.bfloat16), 'head'...  38.2 us
    all_gather x1, blocking collectives, per_device(): lax.all_gather(w_qkv, 'dp', axis=1, tiled=True)  36.7 us
    all_gather x1, waiting for transfers between devices, per_device(): lax.all_gather(held_inputs[3], 'dp', axis=1, tiled=True)  34.4 us
  transfers between devices with their start and end apart: 13, of which 9 were waited for; matrix products, arithmetic and copies ran while one was open for 15% of the time, Pallas kernels for 0%

commit v1 on v0

--- a/solution.py
+++ b/solution.py
@@ -186,7 +186,9 @@
     ).astype(jnp.float32)
     grad_stream = grad_mid + back_attn_norm(grad_normed_attn)[0]
     grad_input = grad_stream[:, :IMG_TOK].astype(jnp.bfloat16)
-    grad_prompts = lax.psum(jnp.sum(grad_stream[:, IMG_TOK:], axis=0), ("dp", "head"))
+    grad_prompts = jnp.sum(
+        lax.all_gather(jnp.sum(grad_stream[:, IMG_TOK:], axis=0), ("dp", "head")), axis=0
+    )
     return (result, grad_input, grad_prompts)
 
 

time: 726 us -> 689 us (0.949)
  waiting for transfers between devices: 379 us -> 337 us
    psum x1 -> x0, waiting for transfers between devices: 122 us -> none  [per_device(): lax.psum(jnp.sum(grad_stream[:, IMG_TOK:], axis=0), ('dp', 'head'))]
    all_gather x0 -> x1, waiting for transfers between devices: none -> 80.2 us  [per_device(): lax.all_gather(jnp.sum(grad_stream[:, IMG_TOK:], axis=0), ('dp', 'head'))]
  transfers between devices with their start and end apart: 13 -> 13, of which waited for: 9 -> 9; matrix products, arithmetic and copies ran while one was open for 15% -> 16% of each run, Pallas kernels for 0% -> 0%
where the time goes in v1:
time: 689 us; the launch traced here: 679 us
  waiting for transfers between devices  337 us (49%)
  blocking collectives  135 us (20%)
  matrix products  132 us (19%)
  other arithmetic  31.6 us (5%)
  local copies, waits for them, and re-layouts  17.1 us (2%)
  between operations  16.4 us (2%)
  starting transfers between devices  9.95 us (1%)
    all_gather x1, waiting for transfers between devices, per_device(): lax.all_gather(jnp.sum(grad_stream[:, IMG_TOK:], axis=0), ('dp', 'head'))  80.2 us
    dot_general x4, matrix products, project(): jnp.einsum('isd,dc->isc', rows_b, weight, preferred_element_type=jnp.floa...  44.9 us
    reduce_scatter x1, waiting for transfers between devices, per_device(): lax.psum_scatter(grad_partial.astype(jnp.bfloat16), 'head', scatter_dimen...  42.3 us
    reduce_scatter x1, waiting for transfers between devices, per_device(): lax.psum_scatter(project(context, full_out).astype(jnp.bfloat16), 'head',...  41.4 us
    all_gather x1, blocking collectives, per_device(): lax.all_gather(held_inputs[0], 'dp', axis=1, tiled=True)  39.4 us
    reduce_scatter x1, waiting for transfers between devices, per_device(): lax.psum_scatter(project(active_b, full_fc2).astype(jnp.bfloat16), 'head'...  38.2 us
    all_gather x1, blocking collectives, per_device(): lax.all_gather(w_qkv, 'dp', axis=1, tiled=True)  36.7 us
    all_gather x1, waiting for transfers between devices, per_device(): lax.all_gather(held_inputs[3], 'dp', axis=1, tiled=True)  34.4 us
  transfers between devices with their start and end apart: 13, of which 9 were waited for; matrix products, arithmetic and copies ran while one was open for 16% of the time, Pallas kernels for 0%

profile of v1, /device:TPU:8, one launch (start us, length us, event | category | flops | bytes accessed | tf_op | source)
XLA Modules:
  0.0 678.7 jit_solution(9835426347474116075)
XLA Ops:
  12.6 36.7 %all_gather.45 = bf16[3,768,192]{2,0,1:T(4,128)(2,1)} all-gather(bf16[3,96,192]{2,0,1:T(4,128)(2,1)S(1)} %copy.34), channel_id=1, replica_groups=mesh['dp'=8,'head'=4] {'dp'}, dimensions={1}, use_global_device_ids=true | all-gather | bytes 995328 | tf_op jit(solution)/shard_map/all_gather | solution.py:120
  52.7 30.5 %all_gather.46 = bf16[192,768]{0,1:T(8,128)(2,1)S(1)} all-gather(bf16[192,96]{0,1:T(8,128)(2,1)S(1)} %copy.37), channel_id=1, replica_groups=mesh['dp'=8,'head'=4] {'dp'}, dimensions={1}, use_global_device_ids=true | all-gather | bytes 331776 | tf_op jit(solution)/shard_map/all_gather | solution.py:121
  90.5 8.2 %fusion.168 = (f32[8,3,297]{2,1,0:T(4,128)S(1)}, f32[8,3,297,297]{2,3,1,0:T(8,128)}) fusion(pred[8,297]{1,0:T(8,128)(4,1)S(1)} %get-tuple-element.30, bf16[8,297,3,64]{1,3,2,0:T(8,128)(2,1)} %bitcast.107, bf16[8,297,3,64]{1,3,2,0:T(8,128)(2,1)} %bitcast.106), kind=kOutput, calls=%fused_computation.222 | convolution fusion | flops 279446432 | bytes 10323720 | tf_op jit(solution)/shard_map/sub | solution.py:43
  98.7 5.8 fusion.73
  110.4 41.4 %reduce-scatter.5.cloned.1.call-done = bf16[2,297,768]{2,1,0:T(8,128)(2,1)} async-done(((bf16[8,297,768]{2,1,0:T(8,128)(2,1)}), bf16[2,297,768]{2,1,0:T(8,128)(2,1)}) %reduce-scatter.5.cloned.1.call-update) | async-done | bytes 912400 | tf_op jit(solution)/shard_map/reduce_scatter | solution.py:138
  161.7 26.8 %all-gather.14.cloned.1.call-done = bf16[8,297,768]{2,1,0:T(8,128)(2,1)} async-done(((bf16[2,297,768]{2,1,0:T(8,128)(2,1)}), bf16[8,297,768]{2,1,0:T(8,128)(2,1)}) %all-gather.14.cloned.1.call-update) | async-done | bytes 3649552 | tf_op jit(solution)/shard_map/all_gather | solution.py:146
  188.5 8.4 %fusion.82 = f32[8,297,768]{2,1,0:T(8,128)} fusion(bf16[8,297,768]{2,1,0:T(8,128)(2,1)} %all-gather.14.cloned.1.call-done, bf16[768,768]{1,0:T(8,128)(2,1)} %all-gather.20.cloned.1.call-done), kind=kOutput, calls=%fused_computation.120 | convolution fusion | flops 2802843648 | bytes 12128256 | tf_op jit(solution)/shard_map/isd,dc->isc/dot_general | solution.py:28
  196.9 34.4 %all-gather.24.cloned.1.call-done = bf16[768,768]{0,1:T(8,128)(2,1)} async-done(((bf16[768,96]{0,1:T(8,128)(2,1)}), bf16[768,768]{0,1:T(8,128)(2,1)}) %all-gather.24.cloned.1.call-update) | async-done | bytes 1179664 | tf_op jit(solution)/shard_map/all_gather | solution.py:159
  231.3 32.9 %all-gather.22.cloned.1.call-done = bf16[8,297,768]{2,1,0:T(8,128)(2,1)} async-done(((bf16[2,297,768]{2,1,0:T(8,128)(2,1)}), bf16[8,297,768]{2,1,0:T(8,128)(2,1)}) %all-gather.22.cloned.1.call-update) | async-done | bytes 3649552 | tf_op jit(solution)/shard_map/all_gather | solution.py:163
  264.2 27.0 %fusion.57 = bf16[8,297,768]{2,1,0:T(8,128)(2,1)} fusion(f32[8,297,768]{2,1,0:T(8,128)} %fusion.82, f32[768]{0:T(1024)S(1)} %copy-done.35, bf16[8,297,768]{2,1,0:T(8,128)(2,1)} %all-gather.22.cloned.1.call-done, bf16[768,768]{0,1:T(8,128)(2,1)} %all-gather.24.cloned.1.call-done, bf16[768,768]{1,0:T(8,128)(2,1)} %all-gather.20.cloned.1.call-done), kind=kOutput, calls=%fused_computation.89 | convolution fusion | flops 5744369664 | bytes 16960512 | tf_op jit(solution)/shard_map/isf,df->isd/dot_general | solution.py:59
  291.2 9.2 %reduce-scatter.7.cloned.1.call-start = ((), (), s32[]{:S(2)}) async-start(), calls=%async_computation.9 | async-start | bytes 4669440 | tf_op jit(solution)/shard_map/reduce_scatter | solution.py:149
  300.4 6.6 all-gather.16.cloned.1.call-done
  307.0 10.3 %fusion.70 = (u8[297,768]{1,0:T(8,128)(4,1)S(1)}, u8[297,768]{1,0:T(8,128)(4,1)S(1)}, f32[8,297,768]{2,1,0:T(8,128)}) fusion(f32[768]{0:T(1024)S(1)} %copy-done.35, bf16[8,297,768]{2,1,0:T(8,128)(2,1)} %all-gather.14.cloned.1.call-done, bf16[768,768]{1,0:T(8,128)(2,1)} %all-gather.16.cloned.1.call-done), kind=kOutput, calls=%fused_computation.109 | convolution fusion | flops 2827934208 | bytes 12587520 | tf_op jit(solution)/shard_map/isd,dc->isc/dot_general | solution.py:28
  317.2 32.0 %all-gather.18.cloned.1.call-done = bf16[768,768]{0,1:T(8,128)(2,1)} async-done(((bf16[768,96]{0,1:T(8,128)(2,1)}), bf16[768,768]{0,1:T(8,128)(2,1)}) %all-gather.18.cloned.1.call-update) | async-done | bytes 1179664 | tf_op jit(solution)/shard_map/all_gather | solution.py:123
  349.3 23.0 %fusion.60 = bf16[8,297,768]{2,1,0:T(8,128)(2,1)} fusion(f32[8,297,768]{2,1,0:T(8,128)} %get-tuple-element.33, f32[768]{0:T(1024)S(1)} %copy-done.35, bf16[768,768]{0,1:T(8,128)(2,1)} %all-gather.18.cloned.1.call-done, u8[297,768]{1,0:T(8,128)(4,1)S(1)} %get-tuple-element.20, u8[297,768]{1,0:T(8,128)(4,1)S(1)} %get-tuple-element.19), kind=kOutput, calls=%fused_computation.90 | convolution fusion | flops 2934226944 | bytes 12587520 | tf_op jit(solution)/shard_map/isd,dc->isc/dot_general | solution.py:28
  375.4 38.2 %reduce-scatter.7.cloned.1.call-done = bf16[2,297,768]{2,1,0:T(8,128)(2,1)} async-done(((bf16[8,297,768]{2,1,0:T(8,128)(2,1)}), bf16[2,297,768]{2,1,0:T(8,128)(2,1)}) %reduce-scatter.7.cloned.1.call-update) | async-done | bytes 912400 | tf_op jit(solution)/shard_map/reduce_scatter | solution.py:149
  417.5 28.5 %all_gather.55 = bf16[192,768]{0,1:T(8,128)(2,1)S(1)} all-gather(bf16[192,96]{0,1:T(8,128)(2,1)S(1)} %copy.42), channel_id=1, replica_groups=mesh['dp'=8,'head'=4] {'dp'}, dimensions={1}, use_global_device_ids=true | all-gather | bytes 331776 | tf_op jit(solution)/shard_map/all_gather | solution.py:157
  446.1 39.4 %all_gather.53 = bf16[3,768,192]{2,0,1:T(4,128)(2,1)S(1)} all-gather(bf16[3,96,192]{2,0,1:T(4,128)(2,1)S(1)} %copy.40), channel_id=1, replica_groups=mesh['dp'=8,'head'=4] {'dp'}, dimensions={1}, use_global_device_ids=true | all-gather | bytes 995328 | tf_op jit(solution)/shard_map/all_gather | solution.py:156
  485.5 7.7 %convert_bitcast_fusion = bf16[3,8,297,192]{2,3,1,0:T(8,128)(2,1)S(1)} fusion(bf16[8,297,768]{2,1,0:T(8,128)(2,1)} %all-gather.12.cloned.1.call-done, bf16[3,768,192,1]{2,0,1,3:T(4,128)(2,1)S(1)} %bitcast.102), kind=kOutput, calls=%fused_computation.84 | convolution fusion | flops 2103501312 | bytes 7271424 | tf_op jit(solution)/shard_map/isd,tdc->tisc/dot_general | solution.py:34
  495.2 8.2 %fusion.169 = (f32[8,3,297]{2,1,0:T(4,128)S(1)}, f32[8,3,297,297]{2,3,1,0:T(8,128)}) fusion(pred[8,297]{1,0:T(8,128)(4,1)S(1)} %copy-done.33, bf16[8,297,3,64]{1,3,2,0:T(8,128)(2,1)} %bitcast.99, bf16[8,297,3,64]{1,3,2,0:T(8,128)(2,1)} %bitcast.97), kind=kOutput, calls=%fused_computation.223 | convolution fusion | flops 279446432 | bytes 10323720 | tf_op jit(solution)/shard_map/sub | solution.py:43
  507.1 7.6 %fusion.74 = bf16[8,3,64,297]{3,2,1,0:T(8,128)(2,1)} fusion(bf16[8,297,3,64]{1,3,2,0:T(8,128)(2,1)S(1)} %bitcast.111, f32[8,3,297,297]{2,3,1,0:T(8,128)} %get-tuple-element.35, f32[8,3,297]{2,1,0:T(4,128)S(1)} %get-tuple-element.34), kind=kOutput, calls=%fused_computation.113 | convolution fusion | flops 275668288 | bytes 10321344 | tf_op jit(solution)/shard_map/ihst,ishc->ithc/dot_general | solution.py:69
  525.0 5.4 bitcast_convert_fusion
  530.5 42.3 %reduce-scatter.11.cloned.1.call-done = bf16[2,297,768]{2,1,0:T(8,128)(2,1)} async-done(((bf16[8,297,768]{2,1,0:T(8,128)(2,1)}), bf16[2,297,768]{2,1,0:T(8,128)(2,1)}) %reduce-scatter.11.cloned.1.call-update) | async-done | bytes 912400 | tf_op jit(solution)/shard_map/reduce_scatter | solution.py:184
  585.8 80.2 %all-gather.28.cloned.1.call-done = f32[32,100,768]{2,1,0:T(8,128)} async-done(((f32[1,100,768]{2,1,0:T(8,128)}), f32[32,100,768]{2,1,0:T(8,128)}) %all-gather.28.cloned.1.call-update) | async-done | bytes 9830416 | tf_op jit(solution)/shard_map/all_gather | solution.py:190
  (159 shorter events, 71.6 us)
Async XLA Ops:
  8.0 75.3 %all-gather.12.cloned.1.call-start = ((), (), s32[]{:S(2)}) async-start(), calls=%async_computation.4 | async-start | bytes 4669440 | tf_op jit(solution)/shard_map/all_gather | solution.py:134
  12.2 71.0 %copy-start.28 = (s32[8,297]{1,0:T(8,128)S(1)}, s32[8,297]{1,0:T(8,128)}, u32[]{:S(2)}) copy-start(s32[8,297]{1,0:T(8,128)} %param.19) | copy-start | bytes 28516
  12.2 71.0 %copy-start.34 = (s32[8]{0:T(128)S(1)}, s32[8]{0:T(128)}, u32[]{:S(2)}) copy-start(s32[8]{0:T(128)} %param.18) | copy-start | bytes 100
  12.2 139.5 %reduce-scatter.5.cloned.1.call-start = ((), (), s32[]{:S(2)}) async-start(), calls=%async_computation.5 | async-start | bytes 4669440 | tf_op jit(solution)/shard_map/reduce_scatter | solution.py:138
  107.7 44.1 %copy-start.12 = (f32[768]{0:T(1024)S(1)}, f32[768]{0:T(1024)}, u32[]{:S(2)}) copy-start(f32[768]{0:T(1024)} %param.24) | copy-start | bytes 9220
  107.7 54.0 %all-gather.20.cloned.1.call-start = ((), (), s32[]{:S(2)}) async-start(), calls=%async_computation.10 | async-start | bytes 1327104 | tf_op jit(solution)/shard_map/all_gather | solution.py:158
  110.3 44.8 %copy-start.17 = (f32[768]{0:T(1024)S(1)}, f32[768]{0:T(1024)}, u32[]{:S(2)}) copy-start(f32[768]{0:T(1024)} %param.25) | copy-start | bytes 9220
  110.3 44.8 %copy-start.30 = (f32[768]{0:T(1024)S(1)}, f32[768]{0:T(1024)}, u32[]{:S(2)}) copy-start(f32[768]{0:T(1024)} %param.26) | copy-start | bytes 9220
  110.3 78.1 %all-gather.14.cloned.1.call-start = ((), (), s32[]{:S(2)}) async-start(), calls=%async_computation.6 | async-start | bytes 4669440 | tf_op jit(solution)/shard_map/all_gather | solution.py:146
  156.6 74.7 %all-gather.24.cloned.1.call-start = ((), (), s32[]{:S(2)}) async-start(), calls=%async_computation.12 | async-start | bytes 1327104 | tf_op jit(solution)/shard_map/all_gather | solution.py:159
  157.2 107.0 %all-gather.22.cloned.1.call-start = ((), (), s32[]{:S(2)}) async-start(), calls=%async_computation.11 | async-start | bytes 4669440 | tf_op jit(solution)/shard_map/all_gather | solution.py:163
  159.9 147.1 %all-gather.16.cloned.1.call-start = ((), (), s32[]{:S(2)}) async-start(), calls=%async_computation.7 | async-start | bytes 1327104 | tf_op jit(solution)/shard_map/all_gather | solution.py:122
  160.6 188.6 %all-gather.18.cloned.1.call-start = ((), (), s32[]{:S(2)}) async-start(), calls=%async_computation.8 | async-start | bytes 1327104 | tf_op jit(solution)/shard_map/all_gather | solution.py:123
  161.4 102.9 %copy-start.35 = (f32[768]{0:T(1024)S(1)}, f32[768]{0:T(1024)}, u32[]{:S(2)}) copy-start(f32[768]{0:T(1024)} %param.28) | copy-start | bytes 9220
  161.4 211.0 %reduce-scatter.9.cloned.1.call-start = ((), (), s32[]{:S(2)}) async-start(), calls=%async_computation.13 | async-start | bytes 4669440 | tf_op jit(solution)/shard_map/reduce_scatter | solution.py:167
  291.2 122.4 %reduce-scatter.7.cloned.1.call-start = ((), (), s32[]{:S(2)}) async-start(), calls=%async_computation.9 | async-start | bytes 4669440 | tf_op jit(solution)/shard_map/reduce_scatter | solution.py:149
  372.3 131.1 %all-gather.26.cloned.1.call-start = ((), (), s32[]{:S(2)}) async-start(), calls=%async_computation.14 | async-start | bytes 4669440 | tf_op jit(solution)/shard_map/all_gather | solution.py:176
  375.4 42.0 %copy-start.11 = (bf16[3,96,192]{2,1,0:T(8,128)(2,1)S(1)}, bf16[3,96,192]{2,1,0:T(8,128)(2,1)}, u32[]{:S(2)}) copy-start(bf16[3,96,192]{2,1,0:T(8,128)(2,1)} %param.22) | copy-start | bytes 331780
  417.2 155.5 %reduce-scatter.11.cloned.1.call-start = ((), (), s32[]{:S(2)}) async-start(), calls=%async_computation.15 | async-start | bytes 4669440 | tf_op jit(solution)/shard_map/reduce_scatter | solution.py:184
  530.4 42.4 %copy-start.16 = (f32[2,297]{1,0:T(2,128)S(1)}, f32[2,297]{1,0:T(2,128)}, u32[]{:S(2)}) copy-start(f32[2,297]{1,0:T(2,128)} %copy-done.15) | copy-start | bytes 7132
  530.4 42.4 %copy-start.19 = (f32[768]{0:T(1024)S(1)}, f32[768]{0:T(1024)}, u32[]{:S(2)}) copy-start(f32[768]{0:T(1024)} %param.20) | copy-start | bytes 9220
  530.4 44.2 %copy-start.25 = (f32[2,297]{1,0:T(2,128)S(1)}, f32[2,297]{1,0:T(2,128)}, u32[]{:S(2)}) copy-start(f32[2,297]{1,0:T(2,128)} %copy-done.24) | copy-start | bytes 7132
  530.4 44.2 %copy-start.21 = (f32[2,297]{1,0:T(2,128)S(1)}, f32[2,297]{1,0:T(2,128)}, u32[]{:S(2)}) copy-start(f32[2,297]{1,0:T(2,128)} %copy-done.20) | copy-start | bytes 7132
  530.4 135.5 %all-gather.28.cloned.1.call-start = ((), (), s32[]{:S(2)}) async-start(), calls=%async_computation.16 | async-start | bytes 10543104 | tf_op jit(solution)/shard_map/all_gather | solution.py:190
  (30 other events, 224.8 us)
Sparse Core Ops, SparseCore 0:
  12.4 33.0 all-gather.11
  107.8 43.8 reduce-scatter.4
  291.3 41.6 reduce-scatter.8
  372.4 41.1 reduce-scatter.6
  580.4 85.4 all-gather.27
Sparse Core Ops, SparseCore 1:
  110.6 42.7 all-gather.19
  156.7 31.7 all-gather.13
  190.8 40.5 all-gather.23
  233.0 31.2 all-gather.21
  266.4 40.5 all-gather.15
  309.2 40.0 all-gather.17
  417.3 31.7 all-gather.25
  530.5 42.2 reduce-scatter.10
